TPU v7x, 512 devices: a whole 4x4x16 slice. The times are simulated.
512 devices in a mesh: lon: 32 (over z, core), lat: 16 (over y, x).
Axes of the slice: x: 4, y: 4, z: 16, core: 2. Of those that a mesh axis runs over, the one named last changes fastest.
Arguments:
- perturbations: float32 [12, 3, 256, 4096], P(None, None, 'lat', 'lon'), as said below
- base_wind: float32 [2, 256, 4096], P(None, 'lat', 'lon'), may hold values from -4 to 4
- base_height: float32 [256, 4096], P('lat', 'lon'), may hold values from 0.5 to 1.5
Outputs:
- fields: float32 [12, 3, 256, 4096], P(None, None, 'lat', 'lon')
- factor: float32 [12, 12], replicated
Inputs may be any that keep to these rules, and one draw needn't show every extreme that they name: `perturbations`: finite real values.
All inputs are finite; a program needn't handle non-finite values.
Results may differ from a plain program's by a relative error of at most 0.00012.
Values sent between devices are 32-bit elements; how exact they have to be, the bound alone decides.
A program may use at most 64 MiB of HBM per device.

v0:
```python
import math
import jax
import jax.numpy as jnp
from jax import lax
from jax.sharding import PartitionSpec as P

STEPS = 8
advect_rate = 0.1
turn_rate = 0.5
gravity_rate = 0.2
diffuse_rate = 0.12


def with_halo(block, sides, width, periodic):
    for axis, dim in sides:
        count = lax.axis_size(axis)
        forward = [(i, i + 1) for i in range(count - 1)]
        if periodic:
            forward.append((count - 1, 0))
        backward = [(target, source) for source, target in forward]
        low = lax.ppermute(
            lax.slice_in_dim(block, block.shape[dim] - width, None, axis=dim), axis, forward
        )
        high = lax.ppermute(lax.slice_in_dim(block, 0, width, axis=dim), axis, backward)
        block = jnp.concatenate([low, block, high], axis=dim)
    return block


def centre(array):
    return array[..., 1:-1, 1:-1]


def diff_lon(array):
    return 0.5 * (array[..., 1:-1, 2:] - array[..., 1:-1, :-2])


def diff_lat(array):
    return 0.5 * (array[..., 2:, 1:-1] - array[..., :-2, 1:-1])


def laplacian(array):
    return (
        array[..., 2:, 1:-1]
        + array[..., :-2, 1:-1]
        + array[..., 1:-1, 2:]
        + array[..., 1:-1, :-2]
        - 4.0 * centre(array)
    )


def advance(field, base, turning):
    wind_x = field[..., 0, :, :]
    wind_y = field[..., 1, :, :]
    height = field[..., 2, :, :]
    base_x = base[0]
    base_y = base[1]
    base_depth = base[2]
    mean_x = centre(base_x)
    mean_y = centre(base_y)
    inner_x = centre(wind_x)
    inner_y = centre(wind_y)
    new_x = (
        inner_x
        - advect_rate
        * (
            mean_x * diff_lon(wind_x)
            + inner_x * diff_lon(base_x)
            + mean_y * diff_lat(wind_x)
            + inner_y * diff_lat(base_x)
        )
        + turn_rate * turning * inner_y
        - gravity_rate * diff_lon(height)
        + diffuse_rate * laplacian(wind_x)
    )
    new_y = (
        inner_y
        - advect_rate
        * (
            mean_x * diff_lon(wind_y)
            + inner_x * diff_lon(base_y)
            + mean_y * diff_lat(wind_y)
            + inner_y * diff_lat(base_y)
        )
        - turn_rate * turning * inner_x
        - gravity_rate * diff_lat(height)
        + diffuse_rate * laplacian(wind_y)
    )
    new_height = (
        centre(height)
        - advect_rate
        * (
            diff_lon(base_depth * wind_x + height * base_x)
            + diff_lat(base_depth * wind_y + height * base_y)
        )
        + diffuse_rate * laplacian(height)
    )
    return jnp.stack([new_x, new_y, new_height], axis=-3)


def coriolis(start, rows, total):
    glob = (start + jnp.arange(rows, dtype=jnp.int32)).astype(jnp.float32)
    return jnp.sin(math.pi * ((glob + 0.5) / total - 0.5))[:, None]


def inside_grid(start, rows, total):
    glob = start + jnp.arange(rows, dtype=jnp.int32)
    return ((glob >= 0) & (glob < total)).astype(jnp.float32)[:, None]


def extend(block, width):
    wide = with_halo(block, (("lon", 3),), width, True)
    return with_halo(wide, (("lat", 2),), width, False)


def per_device(perturbations, base_wind, base_height):
    rows = perturbations.shape[2]
    cols = perturbations.shape[3]
    total_rows = rows * lax.axis_size("lat")
    total_cols = cols * lax.axis_size("lon")
    row_start = lax.axis_index("lat") * rows
    depth = 2
    stacked = jnp.concatenate([base_wind, base_height[None]], axis=0)[None]
    base_ext = extend(stacked, depth)[0]
    field = perturbations
    for group_index in range(STEPS // depth):
        current = extend(field, depth)
        for inner_index in range(depth):
            margin = depth - 1 - inner_index
            turning = coriolis(row_start - margin, rows + 2 * margin, total_rows)
            base_margin = margin + 1
            current = advance(
                current,
                base_ext[
                    :,
                    depth - base_margin : depth + rows + base_margin,
                    depth - base_margin : depth + cols + base_margin,
                ],
                turning,
            )
            if margin > 0:
                current = current * inside_grid(row_start - margin, rows + 2 * margin, total_rows)
        field = current
    flattened = field.reshape(field.shape[0], -1)
    cell_count = float(3 * total_rows * total_cols)
    local_gram = jnp.dot(flattened, flattened.T, precision=lax.Precision.HIGHEST) / cell_count
    gram = lax.psum(local_gram, ("lon", "lat"))
    upper_factor = jnp.linalg.cholesky(gram).T
    lower_factor = upper_factor.T
    fields = jax.scipy.linalg.solve_triangular(lower_factor, flattened, lower=True)
    return (fields.reshape(perturbations.shape), upper_factor)


def solution(mesh):
    return jax.shard_map(
        per_device,
        mesh=mesh,
        in_specs=(P(None, None, "lat", "lon"), P(None, "lat", "lon"), P("lat", "lon")),
        out_specs=(P(None, None, "lat", "lon"), P()),
        check_vma=False,
    )
```

profile of v0, /device:TPU:1, one launch (start us, length us, event | category | flops | bytes accessed | tf_op | source)
XLA Modules:
  0.0 219.9 jit_solution(700765798616330664)
XLA Ops:
  0.6 0.7 maximum_bitcast_fusion
  1.4 3.0 %collective-permute-start.4 = (f32[1,3,16,2]{3,2,1,0:T(8,128)S(1)}, f32[1,3,16,2]{3,2,1,0:T(8,128)S(1)}, u32[]{:S(2)}, u32[]{:S(2)}) collective-permute-start(f32[1,3,16,2]{3,2,1,0:T(8,128)S(1)} %get-tuple-element.82), channel_id=1, source_target_pairs={{0,16},{16,32},{32,48},{48,64},{64,80},{80,96},{96,112},{112,128},... | collective-permute-start | bytes 1160 | tf_op jit(solution)/shard_map/ppermute | solution.py:21
  4.5 3.8 %collective-permute-start.5 = (f32[1,3,16,2]{3,2,1,0:T(8,128)S(1)}, f32[1,3,16,2]{3,2,1,0:T(8,128)S(1)}, u32[]{:S(2)}, u32[]{:S(2)}) collective-permute-start(f32[1,3,16,2]{3,2,1,0:T(8,128)S(1)} %get-tuple-element.83), channel_id=1, source_target_pairs={{16,0},{32,16},{48,32},{64,48},{80,64},{96,80},{112,96},{128,112},... | collective-permute-start | bytes 1160 | tf_op jit(solution)/shard_map/ppermute | solution.py:24
  8.3 1.1 copy.13
  9.6 3.6 %collective-permute-start.1 = (f32[12,3,16,2]{3,0,2,1:T(8,128)S(1)}, f32[12,3,16,2]{3,0,2,1:T(8,128)S(1)}, u32[]{:S(2)}, u32[]{:S(2)}) collective-permute-start(f32[12,3,16,2]{3,0,2,1:T(8,128)S(1)} %get-tuple-element.61), channel_id=1, source_target_pairs={{16,0},{32,16},{48,32},{64,48},{80,64},{96,80},{112,96},{128,112},... | collective-permute-start | bytes 13832 | tf_op jit(solution)/shard_map/ppermute | solution.py:24
  13.3 3.1 %collective-permute-start.6 = (f32[1,3,2,132]{3,2,1,0:T(2,128)S(1)}, f32[1,3,2,132]{3,2,1,0:T(2,128)S(1)}, u32[]{:S(2)}, u32[]{:S(2)}) collective-permute-start(f32[1,3,2,132]{3,2,1,0:T(2,128)S(1)} %get-tuple-element.68), channel_id=1, source_target_pairs={{0,1},{1,2},{2,3},{3,4},{4,5},{5,6},{6,7},{7,8},{8,9},{9,10},{10,1... | collective-permute-start | bytes 9512 | tf_op jit(solution)/shard_map/ppermute | solution.py:21
  16.5 1.3 collective-permute-start.7
  17.8 3.3 %collective-permute-done.7 = f32[1,3,2,132]{3,2,1,0:T(2,128)S(1)} collective-permute-done((f32[1,3,2,132]{3,2,1,0:T(2,128)S(1)}, f32[1,3,2,132]{3,2,1,0:T(2,128)S(1)}, u32[]{:S(2)}, u32[]{:S(2)}) %collective-permute-start.7) | collective-permute-done | bytes 3200 | tf_op jit(solution)/shard_map/ppermute | solution.py:24
  21.7 3.1 %collective-permute-start.2 = (f32[12,3,2,132]{3,0,2,1:T(8,128)S(1)}, f32[12,3,2,132]{3,0,2,1:T(8,128)S(1)}, u32[]{:S(2)}, u32[]{:S(2)}) collective-permute-start(f32[12,3,2,132]{3,0,2,1:T(8,128)S(1)} %get-tuple-element.12), channel_id=1, source_target_pairs={{0,1},{1,2},{2,3},{3,4},{4,5},{5,6},{6,7},{7,8},{8,9},{9,10},{10,1... | collective-permute-start | bytes 114056 | tf_op jit(solution)/shard_map/ppermute | solution.py:21
  24.9 1.3 collective-permute-start.3
  26.5 3.7 %collective-permute-done.3 = f32[12,3,2,132]{3,0,2,1:T(8,128)S(1)} collective-permute-done((f32[12,3,2,132]{3,0,2,1:T(8,128)S(1)}, f32[12,3,2,132]{3,0,2,1:T(8,128)S(1)}, u32[]{:S(2)}, u32[]{:S(2)}) %collective-permute-start.3) | collective-permute-done | bytes 38048 | tf_op jit(solution)/shard_map/ppermute | solution.py:24
  30.2 0.4 pad_maximum_fusion
  30.8 0.6 add_bitcast_fusion.7
  31.4 0.6 add_bitcast_fusion.6
  32.0 0.6 fusion.22
  33.3 0.3 add_bitcast_fusion.14
  33.6 0.3 fusion.42
  34.2 5.5 %collective-permute-start.9 = (f32[12,3,16,2]{3,0,2,1:T(8,128)S(1)}, f32[12,3,16,2]{3,0,2,1:T(8,128)S(1)}, u32[]{:S(2)}, u32[]{:S(2)}) collective-permute-start(f32[12,3,16,2]{3,0,2,1:T(8,128)S(1)} %get-tuple-element.59), channel_id=1, source_target_pairs={{16,0},{32,16},{48,32},{64,48},{80,64},{96,80},{112,96},{128,112},... | collective-permute-start | bytes 13832 | tf_op jit(solution)/shard_map/ppermute | solution.py:24
  39.7 1.2 collective-permute-done.8
  40.9 0.5 collective-permute-done.9
  41.5 4.7 %collective-permute-start.10 = (f32[12,3,2,132]{3,0,2,1:T(8,128)S(1)}, f32[12,3,2,132]{3,0,2,1:T(8,128)S(1)}, u32[]{:S(2)}, u32[]{:S(2)}) collective-permute-start(f32[12,3,2,132]{3,0,2,1:T(8,128)S(1)} %get-tuple-element.10), channel_id=1, source_target_pairs={{0,1},{1,2},{2,3},{3,4},{4,5},{5,6},{6,7},{7,8},{8,9},{9,10},{10,1... | collective-permute-start | bytes 114056 | tf_op jit(solution)/shard_map/ppermute | solution.py:21
  46.2 1.3 collective-permute-start.11
  47.5 0.3 collective-permute-done.10
  47.8 3.7 %collective-permute-done.11 = f32[12,3,2,132]{3,0,2,1:T(8,128)S(1)} collective-permute-done((f32[12,3,2,132]{3,0,2,1:T(8,128)S(1)}, f32[12,3,2,132]{3,0,2,1:T(8,128)S(1)}, u32[]{:S(2)}, u32[]{:S(2)}) %collective-permute-start.11) | collective-permute-done | bytes 38048 | tf_op jit(solution)/shard_map/ppermute | solution.py:24
  51.6 0.4 pad_maximum_fusion.1
  52.0 0.6 add_bitcast_fusion.5
  52.6 0.6 add_bitcast_fusion.4
  53.4 0.6 fusion.17
  54.5 0.3 add_bitcast_fusion.12
  55.0 0.3 fusion.37
  55.5 1.9 collective-permute-start.12
  57.4 6.0 %collective-permute-start.13 = (f32[12,3,16,2]{3,0,2,1:T(8,128)S(1)}, f32[12,3,16,2]{3,0,2,1:T(8,128)S(1)}, u32[]{:S(2)}, u32[]{:S(2)}) collective-permute-start(f32[12,3,16,2]{3,0,2,1:T(8,128)S(1)} %get-tuple-element.57), channel_id=1, source_target_pairs={{16,0},{32,16},{48,32},{64,48},{80,64},{96,80},{112,96},{128,112},... | collective-permute-start | bytes 13832 | tf_op jit(solution)/shard_map/ppermute | solution.py:24
  63.4 1.2 collective-permute-done.12
  64.9 3.8 %collective-permute-start.14 = (f32[12,3,2,132]{3,0,2,1:T(8,128)S(1)}, f32[12,3,2,132]{3,0,2,1:T(8,128)S(1)}, u32[]{:S(2)}, u32[]{:S(2)}) collective-permute-start(f32[12,3,2,132]{3,0,2,1:T(8,128)S(1)} %get-tuple-element.8), channel_id=1, source_target_pairs={{0,1},{1,2},{2,3},{3,4},{4,5},{5,6},{6,7},{7,8},{8,9},{9,10},{10,1... | collective-permute-start | bytes 114056 | tf_op jit(solution)/shard_map/ppermute | solution.py:21
  68.6 1.5 collective-permute-start.15
  70.2 4.0 %collective-permute-done.15 = f32[12,3,2,132]{3,0,2,1:T(8,128)S(1)} collective-permute-done((f32[12,3,2,132]{3,0,2,1:T(8,128)S(1)}, f32[12,3,2,132]{3,0,2,1:T(8,128)S(1)}, u32[]{:S(2)}, u32[]{:S(2)}) %collective-permute-start.15) | collective-permute-done | bytes 38048 | tf_op jit(solution)/shard_map/ppermute | solution.py:24
  74.3 0.4 pad_maximum_fusion.2
  74.7 0.6 add_bitcast_fusion.3
  75.3 0.6 add_bitcast_fusion.2
  76.1 0.6 fusion.12
  77.2 0.3 add_bitcast_fusion.10
  77.6 0.3 fusion.32
  78.2 1.0 collective-permute-start.16
  79.2 7.2 %collective-permute-start.17 = (f32[12,3,16,2]{3,0,2,1:T(8,128)S(1)}, f32[12,3,16,2]{3,0,2,1:T(8,128)S(1)}, u32[]{:S(2)}, u32[]{:S(2)}) collective-permute-start(f32[12,3,16,2]{3,0,2,1:T(8,128)S(1)} %get-tuple-element.55), channel_id=1, source_target_pairs={{16,0},{32,16},{48,32},{64,48},{80,64},{96,80},{112,96},{128,112},... | collective-permute-start | bytes 13832 | tf_op jit(solution)/shard_map/ppermute | solution.py:24
  86.4 1.2 collective-permute-done.16
  87.9 3.8 %collective-permute-start.18 = (f32[12,3,2,132]{3,0,2,1:T(8,128)S(1)}, f32[12,3,2,132]{3,0,2,1:T(8,128)S(1)}, u32[]{:S(2)}, u32[]{:S(2)}) collective-permute-start(f32[12,3,2,132]{3,0,2,1:T(8,128)S(1)} %get-tuple-element.6), channel_id=1, source_target_pairs={{0,1},{1,2},{2,3},{3,4},{4,5},{5,6},{6,7},{7,8},{8,9},{9,10},{10,1... | collective-permute-start | bytes 114056 | tf_op jit(solution)/shard_map/ppermute | solution.py:21
  91.7 1.3 collective-permute-start.19
  93.0 0.3 collective-permute-done.18
  93.3 4.0 %collective-permute-done.19 = f32[12,3,2,132]{3,0,2,1:T(8,128)S(1)} collective-permute-done((f32[12,3,2,132]{3,0,2,1:T(8,128)S(1)}, f32[12,3,2,132]{3,0,2,1:T(8,128)S(1)}, u32[]{:S(2)}, u32[]{:S(2)}) %collective-permute-start.19) | collective-permute-done | bytes 38048 | tf_op jit(solution)/shard_map/ppermute | solution.py:24
  97.3 0.4 pad_maximum_fusion.3
  97.7 0.6 add_bitcast_fusion.1
  98.3 0.6 add_bitcast_fusion
  99.1 0.6 fusion.7
  100.2 0.3 add_bitcast_fusion.8
  100.7 0.3 fusion.27
  101.0 0.6 fusion
  101.7 112.7 %psum.7 = f32[12,12]{0,1:T(8,128)S(1)} all-reduce(f32[12,12]{0,1:T(8,128)S(1)} %fusion), channel_id=1, replica_groups=mesh['lon'=32,'lat'=16] {'lon','lat'}, use_global_device_ids=true, to_apply=%region_0.0 | all-reduce | flops 144 | bytes 1152 | tf_op jit(solution)/shard_map/psum | solution.py:146
  214.4 1.1 cholesky.16
  215.5 0.6 compare_reduce_fusion
  216.2 0.6 fusion.53
  216.9 0.9 custom-call.7
  217.9 0.5 fusion.1
  218.4 0.8 copy.21
  219.2 0.7 copy.22
  (62 shorter events, 6.4 us)
Async XLA Ops:
  1.4 11.8 %collective-permute-start.4 = (f32[1,3,16,2]{3,2,1,0:T(8,128)S(1)}, f32[1,3,16,2]{3,2,1,0:T(8,128)S(1)}, u32[]{:S(2)}, u32[]{:S(2)}) collective-permute-start(f32[1,3,16,2]{3,2,1,0:T(8,128)S(1)} %get-tuple-element.82), channel_id=1, source_target_pairs={{0,16},{16,32},{32,48},{48,64},{64,80},{80,96},{96,112},{112,128},... | collective-permute-start | bytes 1160 | tf_op jit(solution)/shard_map/ppermute | solution.py:21
  4.5 8.8 %collective-permute-start.5 = (f32[1,3,16,2]{3,2,1,0:T(8,128)S(1)}, f32[1,3,16,2]{3,2,1,0:T(8,128)S(1)}, u32[]{:S(2)}, u32[]{:S(2)}) collective-permute-start(f32[1,3,16,2]{3,2,1,0:T(8,128)S(1)} %get-tuple-element.83), channel_id=1, source_target_pairs={{16,0},{32,16},{48,32},{64,48},{80,64},{96,80},{112,96},{128,112},... | collective-permute-start | bytes 1160 | tf_op jit(solution)/shard_map/ppermute | solution.py:24
  9.5 12.0 %collective-permute-start = (f32[12,3,16,2]{3,0,2,1:T(8,128)S(1)}, f32[12,3,16,2]{3,0,2,1:T(8,128)S(1)}, u32[]{:S(2)}, u32[]{:S(2)}) collective-permute-start(f32[12,3,16,2]{3,0,2,1:T(8,128)S(1)} %get-tuple-element.60), channel_id=1, source_target_pairs={{0,16},{16,32},{32,48},{48,64},{64,80},{80,96},{96,112},{112,128},... | collective-permute-start | bytes 13832 | tf_op jit(solution)/shard_map/ppermute | solution.py:21
  9.6 12.0 %collective-permute-start.1 = (f32[12,3,16,2]{3,0,2,1:T(8,128)S(1)}, f32[12,3,16,2]{3,0,2,1:T(8,128)S(1)}, u32[]{:S(2)}, u32[]{:S(2)}) collective-permute-start(f32[12,3,16,2]{3,0,2,1:T(8,128)S(1)} %get-tuple-element.61), channel_id=1, source_target_pairs={{16,0},{32,16},{48,32},{64,48},{80,64},{96,80},{112,96},{128,112},... | collective-permute-start | bytes 13832 | tf_op jit(solution)/shard_map/ppermute | solution.py:24
  13.3 4.5 %collective-permute-start.6 = (f32[1,3,2,132]{3,2,1,0:T(2,128)S(1)}, f32[1,3,2,132]{3,2,1,0:T(2,128)S(1)}, u32[]{:S(2)}, u32[]{:S(2)}) collective-permute-start(f32[1,3,2,132]{3,2,1,0:T(2,128)S(1)} %get-tuple-element.68), channel_id=1, source_target_pairs={{0,1},{1,2},{2,3},{3,4},{4,5},{5,6},{6,7},{7,8},{8,9},{9,10},{10,1... | collective-permute-start | bytes 9512 | tf_op jit(solution)/shard_map/ppermute | solution.py:21
  16.5 4.7 %collective-permute-start.7 = (f32[1,3,2,132]{3,2,1,0:T(2,128)S(1)}, f32[1,3,2,132]{3,2,1,0:T(2,128)S(1)}, u32[]{:S(2)}, u32[]{:S(2)}) collective-permute-start(f32[1,3,2,132]{3,2,1,0:T(2,128)S(1)} %get-tuple-element.69), channel_id=1, source_target_pairs={{1,0},{2,1},{3,2},{4,3},{5,4},{6,5},{7,6},{8,7},{9,8},{10,9},{11,1... | collective-permute-start | bytes 9512 | tf_op jit(solution)/shard_map/ppermute | solution.py:24
  21.7 4.7 %collective-permute-start.2 = (f32[12,3,2,132]{3,0,2,1:T(8,128)S(1)}, f32[12,3,2,132]{3,0,2,1:T(8,128)S(1)}, u32[]{:S(2)}, u32[]{:S(2)}) collective-permute-start(f32[12,3,2,132]{3,0,2,1:T(8,128)S(1)} %get-tuple-element.12), channel_id=1, source_target_pairs={{0,1},{1,2},{2,3},{3,4},{4,5},{5,6},{6,7},{7,8},{8,9},{9,10},{10,1... | collective-permute-start | bytes 114056 | tf_op jit(solution)/shard_map/ppermute | solution.py:21
  24.9 5.4 %collective-permute-start.3 = (f32[12,3,2,132]{3,0,2,1:T(8,128)S(1)}, f32[12,3,2,132]{3,0,2,1:T(8,128)S(1)}, u32[]{:S(2)}, u32[]{:S(2)}) collective-permute-start(f32[12,3,2,132]{3,0,2,1:T(8,128)S(1)} %get-tuple-element.13), channel_id=1, source_target_pairs={{1,0},{2,1},{3,2},{4,3},{5,4},{6,5},{7,6},{8,7},{9,8},{10,9},{11,1... | collective-permute-start | bytes 114056 | tf_op jit(solution)/shard_map/ppermute | solution.py:24
  34.1 6.7 %collective-permute-start.8 = (f32[12,3,16,2]{3,0,2,1:T(8,128)S(1)}, f32[12,3,16,2]{3,0,2,1:T(8,128)S(1)}, u32[]{:S(2)}, u32[]{:S(2)}) collective-permute-start(f32[12,3,16,2]{3,0,2,1:T(8,128)S(1)} %get-tuple-element.58), channel_id=1, source_target_pairs={{0,16},{16,32},{32,48},{48,64},{64,80},{80,96},{96,112},{112,128},... | collective-permute-start | bytes 13832 | tf_op jit(solution)/shard_map/ppermute | solution.py:21
  34.2 7.2 %collective-permute-start.9 = (f32[12,3,16,2]{3,0,2,1:T(8,128)S(1)}, f32[12,3,16,2]{3,0,2,1:T(8,128)S(1)}, u32[]{:S(2)}, u32[]{:S(2)}) collective-permute-start(f32[12,3,16,2]{3,0,2,1:T(8,128)S(1)} %get-tuple-element.59), channel_id=1, source_target_pairs={{16,0},{32,16},{48,32},{64,48},{80,64},{96,80},{112,96},{128,112},... | collective-permute-start | bytes 13832 | tf_op jit(solution)/shard_map/ppermute | solution.py:24
  41.5 6.3 %collective-permute-start.10 = (f32[12,3,2,132]{3,0,2,1:T(8,128)S(1)}, f32[12,3,2,132]{3,0,2,1:T(8,128)S(1)}, u32[]{:S(2)}, u32[]{:S(2)}) collective-permute-start(f32[12,3,2,132]{3,0,2,1:T(8,128)S(1)} %get-tuple-element.10), channel_id=1, source_target_pairs={{0,1},{1,2},{2,3},{3,4},{4,5},{5,6},{6,7},{7,8},{8,9},{9,10},{10,1... | collective-permute-start | bytes 114056 | tf_op jit(solution)/shard_map/ppermute | solution.py:21
  46.2 5.4 %collective-permute-start.11 = (f32[12,3,2,132]{3,0,2,1:T(8,128)S(1)}, f32[12,3,2,132]{3,0,2,1:T(8,128)S(1)}, u32[]{:S(2)}, u32[]{:S(2)}) collective-permute-start(f32[12,3,2,132]{3,0,2,1:T(8,128)S(1)} %get-tuple-element.11), channel_id=1, source_target_pairs={{1,0},{2,1},{3,2},{4,3},{5,4},{6,5},{7,6},{8,7},{9,8},{10,9},{11,1... | collective-permute-start | bytes 114056 | tf_op jit(solution)/shard_map/ppermute | solution.py:24
  55.5 9.1 %collective-permute-start.12 = (f32[12,3,16,2]{3,0,2,1:T(8,128)S(1)}, f32[12,3,16,2]{3,0,2,1:T(8,128)S(1)}, u32[]{:S(2)}, u32[]{:S(2)}) collective-permute-start(f32[12,3,16,2]{3,0,2,1:T(8,128)S(1)} %get-tuple-element.56), channel_id=1, source_target_pairs={{0,16},{16,32},{32,48},{48,64},{64,80},{80,96},{96,112},{112,128},... | collective-permute-start | bytes 13832 | tf_op jit(solution)/shard_map/ppermute | solution.py:21
  57.4 7.4 %collective-permute-start.13 = (f32[12,3,16,2]{3,0,2,1:T(8,128)S(1)}, f32[12,3,16,2]{3,0,2,1:T(8,128)S(1)}, u32[]{:S(2)}, u32[]{:S(2)}) collective-permute-start(f32[12,3,16,2]{3,0,2,1:T(8,128)S(1)} %get-tuple-element.57), channel_id=1, source_target_pairs={{16,0},{32,16},{48,32},{64,48},{80,64},{96,80},{112,96},{128,112},... | collective-permute-start | bytes 13832 | tf_op jit(solution)/shard_map/ppermute | solution.py:24
  64.9 5.4 %collective-permute-start.14 = (f32[12,3,2,132]{3,0,2,1:T(8,128)S(1)}, f32[12,3,2,132]{3,0,2,1:T(8,128)S(1)}, u32[]{:S(2)}, u32[]{:S(2)}) collective-permute-start(f32[12,3,2,132]{3,0,2,1:T(8,128)S(1)} %get-tuple-element.8), channel_id=1, source_target_pairs={{0,1},{1,2},{2,3},{3,4},{4,5},{5,6},{6,7},{7,8},{8,9},{9,10},{10,1... | collective-permute-start | bytes 114056 | tf_op jit(solution)/shard_map/ppermute | solution.py:21
  68.6 5.6 %collective-permute-start.15 = (f32[12,3,2,132]{3,0,2,1:T(8,128)S(1)}, f32[12,3,2,132]{3,0,2,1:T(8,128)S(1)}, u32[]{:S(2)}, u32[]{:S(2)}) collective-permute-start(f32[12,3,2,132]{3,0,2,1:T(8,128)S(1)} %get-tuple-element.9), channel_id=1, source_target_pairs={{1,0},{2,1},{3,2},{4,3},{5,4},{6,5},{7,6},{8,7},{9,8},{10,9},{11,1... | collective-permute-start | bytes 114056 | tf_op jit(solution)/shard_map/ppermute | solution.py:24
  78.2 9.4 %collective-permute-start.16 = (f32[12,3,16,2]{3,0,2,1:T(8,128)S(1)}, f32[12,3,16,2]{3,0,2,1:T(8,128)S(1)}, u32[]{:S(2)}, u32[]{:S(2)}) collective-permute-start(f32[12,3,16,2]{3,0,2,1:T(8,128)S(1)} %get-tuple-element.54), channel_id=1, source_target_pairs={{0,16},{16,32},{32,48},{48,64},{64,80},{80,96},{96,112},{112,128},... | collective-permute-start | bytes 13832 | tf_op jit(solution)/shard_map/ppermute | solution.py:21
  79.2 8.6 %collective-permute-start.17 = (f32[12,3,16,2]{3,0,2,1:T(8,128)S(1)}, f32[12,3,16,2]{3,0,2,1:T(8,128)S(1)}, u32[]{:S(2)}, u32[]{:S(2)}) collective-permute-start(f32[12,3,16,2]{3,0,2,1:T(8,128)S(1)} %get-tuple-element.55), channel_id=1, source_target_pairs={{16,0},{32,16},{48,32},{64,48},{80,64},{96,80},{112,96},{128,112},... | collective-permute-start | bytes 13832 | tf_op jit(solution)/shard_map/ppermute | solution.py:24
  87.9 5.4 %collective-permute-start.18 = (f32[12,3,2,132]{3,0,2,1:T(8,128)S(1)}, f32[12,3,2,132]{3,0,2,1:T(8,128)S(1)}, u32[]{:S(2)}, u32[]{:S(2)}) collective-permute-start(f32[12,3,2,132]{3,0,2,1:T(8,128)S(1)} %get-tuple-element.6), channel_id=1, source_target_pairs={{0,1},{1,2},{2,3},{3,4},{4,5},{5,6},{6,7},{7,8},{8,9},{9,10},{10,1... | collective-permute-start | bytes 114056 | tf_op jit(solution)/shard_map/ppermute | solution.py:21
  91.7 5.6 %collective-permute-start.19 = (f32[12,3,2,132]{3,0,2,1:T(8,128)S(1)}, f32[12,3,2,132]{3,0,2,1:T(8,128)S(1)}, u32[]{:S(2)}, u32[]{:S(2)}) collective-permute-start(f32[12,3,2,132]{3,0,2,1:T(8,128)S(1)} %get-tuple-element.7), channel_id=1, source_target_pairs={{1,0},{2,1},{3,2},{4,3},{5,4},{6,5},{7,6},{8,7},{9,8},{10,9},{11,1... | collective-permute-start | bytes 114056 | tf_op jit(solution)/shard_map/ppermute | solution.py:24
where the time goes:
time: 221 us; the launch traced here: 220 us
  blocking collectives  113 us (51%)
  starting transfers between devices  57.2 us (26%)
  waiting for transfers between devices  24.3 us (11%)
  other arithmetic  19.3 us (9%)
  local copies, waits for them, and re-layouts  4.13 us (2%)
    psum x1, blocking collectives, per_device(): gram = lax.psum(local_gram, ('lon', 'lat'))  113 us
    ppermute x10, starting transfers between devices, with_halo(): lax.ppermute(lax.slice_in_dim(block, 0, width, axis=dim), axis, backward)  32.8 us
    ppermute x10, starting transfers between devices, with_halo(): lax.ppermute(lax.slice_in_dim(block, block.shape[dim] - width, None, axis...  24.4 us
    ppermute x10, waiting for transfers between devices, with_halo(): lax.ppermute(lax.slice_in_dim(block, 0, width, axis=dim), axis, backward)  19.7 us
    another operation x28, other arithmetic, advance(): return jnp.stack([new_x, new_y, new_height], axis=-3)  11 us
    ppermute x10, waiting for transfers between devices, with_halo(): lax.ppermute(lax.slice_in_dim(block, block.shape[dim] - width, None, axis...  4.58 us
  transfers between devices with their start and end apart: 20, of which 15 were waited for; matrix products, arithmetic and copies ran while one was open for 1% of the time, Pallas kernels for 0%

commit v1 on v0

--- a/solution.py
+++ b/solution.py
@@ -143,7 +143,7 @@
     flattened = field.reshape(field.shape[0], -1)
     cell_count = float(3 * total_rows * total_cols)
     local_gram = jnp.dot(flattened, flattened.T, precision=lax.Precision.HIGHEST) / cell_count
-    gram = lax.psum(local_gram, ("lon", "lat"))
+    gram = lax.psum(lax.psum(local_gram, "lat"), "lon")
     upper_factor = jnp.linalg.cholesky(gram).T
     lower_factor = upper_factor.T
     fields = jax.scipy.linalg.solve_triangular(lower_factor, flattened, lower=True)

time: 221 us -> 200 us (0.905)
  blocking collectives: 113 us -> 92.4 us
    psum x1 -> x2, blocking collectives: 113 us -> 92.4 us  [per_device(): gram = lax.psum(lax.psum(local_gram, 'lat'), 'lon')]
where the time goes in v1:
time: 200 us
  blocking collectives  92.4 us (46%)
  starting transfers between devices  57.2 us (29%)
  waiting for transfers between devices  24.3 us (12%)
  other arithmetic  19.3 us (10%)
  local copies, waits for them, and re-layouts  4.13 us (2%)
    psum x2, blocking collectives, per_device(): gram = lax.psum(lax.psum(local_gram, 'lat'), 'lon')  92.4 us
    ppermute x10, starting transfers between devices, with_halo(): lax.ppermute(lax.slice_in_dim(block, 0, width, axis=dim), axis, backward)  32.8 us
    ppermute x10, starting transfers between devices, with_halo(): lax.ppermute(lax.slice_in_dim(block, block.shape[dim] - width, None, axis...  24.4 us
    ppermute x10, waiting for transfers between devices, with_halo(): lax.ppermute(lax.slice_in_dim(block, 0, width, axis=dim), axis, backward)  19.7 us
    another operation x28, other arithmetic, advance(): return jnp.stack([new_x, new_y, new_height], axis=-3)  11 us
    ppermute x10, waiting for transfers between devices, with_halo(): lax.ppermute(lax.slice_in_dim(block, block.shape[dim] - width, None, axis...  4.58 us
  transfers between devices with their start and end apart: 20, of which 15 were waited for; matrix products, arithmetic and copies ran while one was open for 1% of the time, Pallas kernels for 0%

profile of v1, /device:TPU:1, one launch (start us, length us, event | category | flops | bytes accessed | tf_op | source)
XLA Modules:
  0.0 199.7 jit_solution(16429894164492371721)
XLA Ops:
  0.6 0.7 maximum_bitcast_fusion
  1.4 3.0 %collective-permute-start.4 = (f32[1,3,16,2]{3,2,1,0:T(8,128)S(1)}, f32[1,3,16,2]{3,2,1,0:T(8,128)S(1)}, u32[]{:S(2)}, u32[]{:S(2)}) collective-permute-start(f32[1,3,16,2]{3,2,1,0:T(8,128)S(1)} %get-tuple-element.82), channel_id=1, source_target_pairs={{0,16},{16,32},{32,48},{48,64},{64,80},{80,96},{96,112},{112,128},... | collective-permute-start | bytes 1160 | tf_op jit(solution)/shard_map/ppermute | solution.py:21
  4.5 3.8 %collective-permute-start.5 = (f32[1,3,16,2]{3,2,1,0:T(8,128)S(1)}, f32[1,3,16,2]{3,2,1,0:T(8,128)S(1)}, u32[]{:S(2)}, u32[]{:S(2)}) collective-permute-start(f32[1,3,16,2]{3,2,1,0:T(8,128)S(1)} %get-tuple-element.83), channel_id=1, source_target_pairs={{16,0},{32,16},{48,32},{64,48},{80,64},{96,80},{112,96},{128,112},... | collective-permute-start | bytes 1160 | tf_op jit(solution)/shard_map/ppermute | solution.py:24
  8.3 1.1 copy.13
  9.6 3.6 %collective-permute-start.1 = (f32[12,3,16,2]{3,0,2,1:T(8,128)S(1)}, f32[12,3,16,2]{3,0,2,1:T(8,128)S(1)}, u32[]{:S(2)}, u32[]{:S(2)}) collective-permute-start(f32[12,3,16,2]{3,0,2,1:T(8,128)S(1)} %get-tuple-element.61), channel_id=1, source_target_pairs={{16,0},{32,16},{48,32},{64,48},{80,64},{96,80},{112,96},{128,112},... | collective-permute-start | bytes 13832 | tf_op jit(solution)/shard_map/ppermute | solution.py:24
  13.3 3.1 %collective-permute-start.6 = (f32[1,3,2,132]{3,2,1,0:T(2,128)S(1)}, f32[1,3,2,132]{3,2,1,0:T(2,128)S(1)}, u32[]{:S(2)}, u32[]{:S(2)}) collective-permute-start(f32[1,3,2,132]{3,2,1,0:T(2,128)S(1)} %get-tuple-element.68), channel_id=1, source_target_pairs={{0,1},{1,2},{2,3},{3,4},{4,5},{5,6},{6,7},{7,8},{8,9},{9,10},{10,1... | collective-permute-start | bytes 9512 | tf_op jit(solution)/shard_map/ppermute | solution.py:21
  16.5 1.3 collective-permute-start.7
  17.8 3.3 %collective-permute-done.7 = f32[1,3,2,132]{3,2,1,0:T(2,128)S(1)} collective-permute-done((f32[1,3,2,132]{3,2,1,0:T(2,128)S(1)}, f32[1,3,2,132]{3,2,1,0:T(2,128)S(1)}, u32[]{:S(2)}, u32[]{:S(2)}) %collective-permute-start.7) | collective-permute-done | bytes 3200 | tf_op jit(solution)/shard_map/ppermute | solution.py:24
  21.7 3.1 %collective-permute-start.2 = (f32[12,3,2,132]{3,0,2,1:T(8,128)S(1)}, f32[12,3,2,132]{3,0,2,1:T(8,128)S(1)}, u32[]{:S(2)}, u32[]{:S(2)}) collective-permute-start(f32[12,3,2,132]{3,0,2,1:T(8,128)S(1)} %get-tuple-element.12), channel_id=1, source_target_pairs={{0,1},{1,2},{2,3},{3,4},{4,5},{5,6},{6,7},{7,8},{8,9},{9,10},{10,1... | collective-permute-start | bytes 114056 | tf_op jit(solution)/shard_map/ppermute | solution.py:21
  24.9 1.3 collective-permute-start.3
  26.5 3.7 %collective-permute-done.3 = f32[12,3,2,132]{3,0,2,1:T(8,128)S(1)} collective-permute-done((f32[12,3,2,132]{3,0,2,1:T(8,128)S(1)}, f32[12,3,2,132]{3,0,2,1:T(8,128)S(1)}, u32[]{:S(2)}, u32[]{:S(2)}) %collective-permute-start.3) | collective-permute-done | bytes 38048 | tf_op jit(solution)/shard_map/ppermute | solution.py:24
  30.2 0.4 pad_maximum_fusion
  30.8 0.6 add_bitcast_fusion.7
  31.4 0.6 add_bitcast_fusion.6
  32.0 0.6 fusion.22
  33.3 0.3 add_bitcast_fusion.14
  33.6 0.3 fusion.42
  34.2 5.5 %collective-permute-start.9 = (f32[12,3,16,2]{3,0,2,1:T(8,128)S(1)}, f32[12,3,16,2]{3,0,2,1:T(8,128)S(1)}, u32[]{:S(2)}, u32[]{:S(2)}) collective-permute-start(f32[12,3,16,2]{3,0,2,1:T(8,128)S(1)} %get-tuple-element.59), channel_id=1, source_target_pairs={{16,0},{32,16},{48,32},{64,48},{80,64},{96,80},{112,96},{128,112},... | collective-permute-start | bytes 13832 | tf_op jit(solution)/shard_map/ppermute | solution.py:24
  39.7 1.2 collective-permute-done.8
  40.9 0.5 collective-permute-done.9
  41.5 4.7 %collective-permute-start.10 = (f32[12,3,2,132]{3,0,2,1:T(8,128)S(1)}, f32[12,3,2,132]{3,0,2,1:T(8,128)S(1)}, u32[]{:S(2)}, u32[]{:S(2)}) collective-permute-start(f32[12,3,2,132]{3,0,2,1:T(8,128)S(1)} %get-tuple-element.10), channel_id=1, source_target_pairs={{0,1},{1,2},{2,3},{3,4},{4,5},{5,6},{6,7},{7,8},{8,9},{9,10},{10,1... | collective-permute-start | bytes 114056 | tf_op jit(solution)/shard_map/ppermute | solution.py:21
  46.2 1.3 collective-permute-start.11
  47.5 0.3 collective-permute-done.10
  47.8 3.7 %collective-permute-done.11 = f32[12,3,2,132]{3,0,2,1:T(8,128)S(1)} collective-permute-done((f32[12,3,2,132]{3,0,2,1:T(8,128)S(1)}, f32[12,3,2,132]{3,0,2,1:T(8,128)S(1)}, u32[]{:S(2)}, u32[]{:S(2)}) %collective-permute-start.11) | collective-permute-done | bytes 38048 | tf_op jit(solution)/shard_map/ppermute | solution.py:24
  51.6 0.4 pad_maximum_fusion.1
  52.0 0.6 add_bitcast_fusion.5
  52.6 0.6 add_bitcast_fusion.4
  53.4 0.6 fusion.17
  54.5 0.3 add_bitcast_fusion.12
  55.0 0.3 fusion.37
  55.5 1.9 collective-permute-start.12
  57.4 6.0 %collective-permute-start.13 = (f32[12,3,16,2]{3,0,2,1:T(8,128)S(1)}, f32[12,3,16,2]{3,0,2,1:T(8,128)S(1)}, u32[]{:S(2)}, u32[]{:S(2)}) collective-permute-start(f32[12,3,16,2]{3,0,2,1:T(8,128)S(1)} %get-tuple-element.57), channel_id=1, source_target_pairs={{16,0},{32,16},{48,32},{64,48},{80,64},{96,80},{112,96},{128,112},... | collective-permute-start | bytes 13832 | tf_op jit(solution)/shard_map/ppermute | solution.py:24
  63.4 1.2 collective-permute-done.12
  64.9 3.8 %collective-permute-start.14 = (f32[12,3,2,132]{3,0,2,1:T(8,128)S(1)}, f32[12,3,2,132]{3,0,2,1:T(8,128)S(1)}, u32[]{:S(2)}, u32[]{:S(2)}) collective-permute-start(f32[12,3,2,132]{3,0,2,1:T(8,128)S(1)} %get-tuple-element.8), channel_id=1, source_target_pairs={{0,1},{1,2},{2,3},{3,4},{4,5},{5,6},{6,7},{7,8},{8,9},{9,10},{10,1... | collective-permute-start | bytes 114056 | tf_op jit(solution)/shard_map/ppermute | solution.py:21
  68.6 1.5 collective-permute-start.15
  70.2 4.0 %collective-permute-done.15 = f32[12,3,2,132]{3,0,2,1:T(8,128)S(1)} collective-permute-done((f32[12,3,2,132]{3,0,2,1:T(8,128)S(1)}, f32[12,3,2,132]{3,0,2,1:T(8,128)S(1)}, u32[]{:S(2)}, u32[]{:S(2)}) %collective-permute-start.15) | collective-permute-done | bytes 38048 | tf_op jit(solution)/shard_map/ppermute | solution.py:24
  74.3 0.4 pad_maximum_fusion.2
  74.7 0.6 add_bitcast_fusion.3
  75.3 0.6 add_bitcast_fusion.2
  76.1 0.6 fusion.12
  77.2 0.3 add_bitcast_fusion.10
  77.6 0.3 fusion.32
  78.2 1.0 collective-permute-start.16
  79.2 7.2 %collective-permute-start.17 = (f32[12,3,16,2]{3,0,2,1:T(8,128)S(1)}, f32[12,3,16,2]{3,0,2,1:T(8,128)S(1)}, u32[]{:S(2)}, u32[]{:S(2)}) collective-permute-start(f32[12,3,16,2]{3,0,2,1:T(8,128)S(1)} %get-tuple-element.55), channel_id=1, source_target_pairs={{16,0},{32,16},{48,32},{64,48},{80,64},{96,80},{112,96},{128,112},... | collective-permute-start | bytes 13832 | tf_op jit(solution)/shard_map/ppermute | solution.py:24
  86.4 1.2 collective-permute-done.16
  87.9 3.8 %collective-permute-start.18 = (f32[12,3,2,132]{3,0,2,1:T(8,128)S(1)}, f32[12,3,2,132]{3,0,2,1:T(8,128)S(1)}, u32[]{:S(2)}, u32[]{:S(2)}) collective-permute-start(f32[12,3,2,132]{3,0,2,1:T(8,128)S(1)} %get-tuple-element.6), channel_id=1, source_target_pairs={{0,1},{1,2},{2,3},{3,4},{4,5},{5,6},{6,7},{7,8},{8,9},{9,10},{10,1... | collective-permute-start | bytes 114056 | tf_op jit(solution)/shard_map/ppermute | solution.py:21
  91.7 1.3 collective-permute-start.19
  93.0 0.3 collective-permute-done.18
  93.3 4.0 %collective-permute-done.19 = f32[12,3,2,132]{3,0,2,1:T(8,128)S(1)} collective-permute-done((f32[12,3,2,132]{3,0,2,1:T(8,128)S(1)}, f32[12,3,2,132]{3,0,2,1:T(8,128)S(1)}, u32[]{:S(2)}, u32[]{:S(2)}) %collective-permute-start.19) | collective-permute-done | bytes 38048 | tf_op jit(solution)/shard_map/ppermute | solution.py:24
  97.3 0.4 pad_maximum_fusion.3
  97.7 0.6 add_bitcast_fusion.1
  98.3 0.6 add_bitcast_fusion
  99.1 0.6 fusion.7
  100.2 0.3 add_bitcast_fusion.8
  101.0 0.6 fusion
  101.7 30.9 %psum.14 = f32[12,12]{0,1:T(8,128)S(1)} all-reduce(f32[12,12]{0,1:T(8,128)S(1)} %fusion), channel_id=1, replica_groups=mesh['lon'=32,'lat'=16] {'lat'}, use_global_device_ids=true, to_apply=%region_0.0 | all-reduce | flops 144 | bytes 1152 | tf_op jit(solution)/shard_map/psum | solution.py:146
  132.6 61.5 %psum.15 = f32[12,12]{0,1:T(8,128)S(1)} all-reduce(f32[12,12]{0,1:T(8,128)S(1)} %psum.14), channel_id=1, replica_groups=mesh['lon'=32,'lat'=16] {'lon'}, use_global_device_ids=true, to_apply=%region_1.0 | all-reduce | flops 144 | bytes 1152 | tf_op jit(solution)/shard_map/psum | solution.py:146
  194.2 1.1 cholesky.16
  195.3 0.6 compare_reduce_fusion
  196.0 0.6 fusion.53
  196.6 0.9 custom-call.7
  197.7 0.5 fusion.1
  198.2 0.8 copy.21
  199.0 0.7 copy.22
  (63 shorter events, 6.7 us)
Async XLA Ops:
  1.4 11.8 %collective-permute-start.4 = (f32[1,3,16,2]{3,2,1,0:T(8,128)S(1)}, f32[1,3,16,2]{3,2,1,0:T(8,128)S(1)}, u32[]{:S(2)}, u32[]{:S(2)}) collective-permute-start(f32[1,3,16,2]{3,2,1,0:T(8,128)S(1)} %get-tuple-element.82), channel_id=1, source_target_pairs={{0,16},{16,32},{32,48},{48,64},{64,80},{80,96},{96,112},{112,128},... | collective-permute-start | bytes 1160 | tf_op jit(solution)/shard_map/ppermute | solution.py:21
  4.5 8.8 %collective-permute-start.5 = (f32[1,3,16,2]{3,2,1,0:T(8,128)S(1)}, f32[1,3,16,2]{3,2,1,0:T(8,128)S(1)}, u32[]{:S(2)}, u32[]{:S(2)}) collective-permute-start(f32[1,3,16,2]{3,2,1,0:T(8,128)S(1)} %get-tuple-element.83), channel_id=1, source_target_pairs={{16,0},{32,16},{48,32},{64,48},{80,64},{96,80},{112,96},{128,112},... | collective-permute-start | bytes 1160 | tf_op jit(solution)/shard_map/ppermute | solution.py:24
  9.5 12.0 %collective-permute-start = (f32[12,3,16,2]{3,0,2,1:T(8,128)S(1)}, f32[12,3,16,2]{3,0,2,1:T(8,128)S(1)}, u32[]{:S(2)}, u32[]{:S(2)}) collective-permute-start(f32[12,3,16,2]{3,0,2,1:T(8,128)S(1)} %get-tuple-element.60), channel_id=1, source_target_pairs={{0,16},{16,32},{32,48},{48,64},{64,80},{80,96},{96,112},{112,128},... | collective-permute-start | bytes 13832 | tf_op jit(solution)/shard_map/ppermute | solution.py:21
  9.6 12.0 %collective-permute-start.1 = (f32[12,3,16,2]{3,0,2,1:T(8,128)S(1)}, f32[12,3,16,2]{3,0,2,1:T(8,128)S(1)}, u32[]{:S(2)}, u32[]{:S(2)}) collective-permute-start(f32[12,3,16,2]{3,0,2,1:T(8,128)S(1)} %get-tuple-element.61), channel_id=1, source_target_pairs={{16,0},{32,16},{48,32},{64,48},{80,64},{96,80},{112,96},{128,112},... | collective-permute-start | bytes 13832 | tf_op jit(solution)/shard_map/ppermute | solution.py:24
  13.3 4.5 %collective-permute-start.6 = (f32[1,3,2,132]{3,2,1,0:T(2,128)S(1)}, f32[1,3,2,132]{3,2,1,0:T(2,128)S(1)}, u32[]{:S(2)}, u32[]{:S(2)}) collective-permute-start(f32[1,3,2,132]{3,2,1,0:T(2,128)S(1)} %get-tuple-element.68), channel_id=1, source_target_pairs={{0,1},{1,2},{2,3},{3,4},{4,5},{5,6},{6,7},{7,8},{8,9},{9,10},{10,1... | collective-permute-start | bytes 9512 | tf_op jit(solution)/shard_map/ppermute | solution.py:21
  16.5 4.7 %collective-permute-start.7 = (f32[1,3,2,132]{3,2,1,0:T(2,128)S(1)}, f32[1,3,2,132]{3,2,1,0:T(2,128)S(1)}, u32[]{:S(2)}, u32[]{:S(2)}) collective-permute-start(f32[1,3,2,132]{3,2,1,0:T(2,128)S(1)} %get-tuple-element.69), channel_id=1, source_target_pairs={{1,0},{2,1},{3,2},{4,3},{5,4},{6,5},{7,6},{8,7},{9,8},{10,9},{11,1... | collective-permute-start | bytes 9512 | tf_op jit(solution)/shard_map/ppermute | solution.py:24
  21.7 4.7 %collective-permute-start.2 = (f32[12,3,2,132]{3,0,2,1:T(8,128)S(1)}, f32[12,3,2,132]{3,0,2,1:T(8,128)S(1)}, u32[]{:S(2)}, u32[]{:S(2)}) collective-permute-start(f32[12,3,2,132]{3,0,2,1:T(8,128)S(1)} %get-tuple-element.12), channel_id=1, source_target_pairs={{0,1},{1,2},{2,3},{3,4},{4,5},{5,6},{6,7},{7,8},{8,9},{9,10},{10,1... | collective-permute-start | bytes 114056 | tf_op jit(solution)/shard_map/ppermute | solution.py:21
  24.9 5.4 %collective-permute-start.3 = (f32[12,3,2,132]{3,0,2,1:T(8,128)S(1)}, f32[12,3,2,132]{3,0,2,1:T(8,128)S(1)}, u32[]{:S(2)}, u32[]{:S(2)}) collective-permute-start(f32[12,3,2,132]{3,0,2,1:T(8,128)S(1)} %get-tuple-element.13), channel_id=1, source_target_pairs={{1,0},{2,1},{3,2},{4,3},{5,4},{6,5},{7,6},{8,7},{9,8},{10,9},{11,1... | collective-permute-start | bytes 114056 | tf_op jit(solution)/shard_map/ppermute | solution.py:24
  34.1 6.7 %collective-permute-start.8 = (f32[12,3,16,2]{3,0,2,1:T(8,128)S(1)}, f32[12,3,16,2]{3,0,2,1:T(8,128)S(1)}, u32[]{:S(2)}, u32[]{:S(2)}) collective-permute-start(f32[12,3,16,2]{3,0,2,1:T(8,128)S(1)} %get-tuple-element.58), channel_id=1, source_target_pairs={{0,16},{16,32},{32,48},{48,64},{64,80},{80,96},{96,112},{112,128},... | collective-permute-start | bytes 13832 | tf_op jit(solution)/shard_map/ppermute | solution.py:21
  34.2 7.2 %collective-permute-start.9 = (f32[12,3,16,2]{3,0,2,1:T(8,128)S(1)}, f32[12,3,16,2]{3,0,2,1:T(8,128)S(1)}, u32[]{:S(2)}, u32[]{:S(2)}) collective-permute-start(f32[12,3,16,2]{3,0,2,1:T(8,128)S(1)} %get-tuple-element.59), channel_id=1, source_target_pairs={{16,0},{32,16},{48,32},{64,48},{80,64},{96,80},{112,96},{128,112},... | collective-permute-start | bytes 13832 | tf_op jit(solution)/shard_map/ppermute | solution.py:24
  41.5 6.3 %collective-permute-start.10 = (f32[12,3,2,132]{3,0,2,1:T(8,128)S(1)}, f32[12,3,2,132]{3,0,2,1:T(8,128)S(1)}, u32[]{:S(2)}, u32[]{:S(2)}) collective-permute-start(f32[12,3,2,132]{3,0,2,1:T(8,128)S(1)} %get-tuple-element.10), channel_id=1, source_target_pairs={{0,1},{1,2},{2,3},{3,4},{4,5},{5,6},{6,7},{7,8},{8,9},{9,10},{10,1... | collective-permute-start | bytes 114056 | tf_op jit(solution)/shard_map/ppermute | solution.py:21
  46.2 5.4 %collective-permute-start.11 = (f32[12,3,2,132]{3,0,2,1:T(8,128)S(1)}, f32[12,3,2,132]{3,0,2,1:T(8,128)S(1)}, u32[]{:S(2)}, u32[]{:S(2)}) collective-permute-start(f32[12,3,2,132]{3,0,2,1:T(8,128)S(1)} %get-tuple-element.11), channel_id=1, source_target_pairs={{1,0},{2,1},{3,2},{4,3},{5,4},{6,5},{7,6},{8,7},{9,8},{10,9},{11,1... | collective-permute-start | bytes 114056 | tf_op jit(solution)/shard_map/ppermute | solution.py:24
  55.5 9.1 %collective-permute-start.12 = (f32[12,3,16,2]{3,0,2,1:T(8,128)S(1)}, f32[12,3,16,2]{3,0,2,1:T(8,128)S(1)}, u32[]{:S(2)}, u32[]{:S(2)}) collective-permute-start(f32[12,3,16,2]{3,0,2,1:T(8,128)S(1)} %get-tuple-element.56), channel_id=1, source_target_pairs={{0,16},{16,32},{32,48},{48,64},{64,80},{80,96},{96,112},{112,128},... | collective-permute-start | bytes 13832 | tf_op jit(solution)/shard_map/ppermute | solution.py:21
  57.4 7.4 %collective-permute-start.13 = (f32[12,3,16,2]{3,0,2,1:T(8,128)S(1)}, f32[12,3,16,2]{3,0,2,1:T(8,128)S(1)}, u32[]{:S(2)}, u32[]{:S(2)}) collective-permute-start(f32[12,3,16,2]{3,0,2,1:T(8,128)S(1)} %get-tuple-element.57), channel_id=1, source_target_pairs={{16,0},{32,16},{48,32},{64,48},{80,64},{96,80},{112,96},{128,112},... | collective-permute-start | bytes 13832 | tf_op jit(solution)/shard_map/ppermute | solution.py:24
  64.9 5.4 %collective-permute-start.14 = (f32[12,3,2,132]{3,0,2,1:T(8,128)S(1)}, f32[12,3,2,132]{3,0,2,1:T(8,128)S(1)}, u32[]{:S(2)}, u32[]{:S(2)}) collective-permute-start(f32[12,3,2,132]{3,0,2,1:T(8,128)S(1)} %get-tuple-element.8), channel_id=1, source_target_pairs={{0,1},{1,2},{2,3},{3,4},{4,5},{5,6},{6,7},{7,8},{8,9},{9,10},{10,1... | collective-permute-start | bytes 114056 | tf_op jit(solution)/shard_map/ppermute | solution.py:21
  68.6 5.6 %collective-permute-start.15 = (f32[12,3,2,132]{3,0,2,1:T(8,128)S(1)}, f32[12,3,2,132]{3,0,2,1:T(8,128)S(1)}, u32[]{:S(2)}, u32[]{:S(2)}) collective-permute-start(f32[12,3,2,132]{3,0,2,1:T(8,128)S(1)} %get-tuple-element.9), channel_id=1, source_target_pairs={{1,0},{2,1},{3,2},{4,3},{5,4},{6,5},{7,6},{8,7},{9,8},{10,9},{11,1... | collective-permute-start | bytes 114056 | tf_op jit(solution)/shard_map/ppermute | solution.py:24
  78.2 9.4 %collective-permute-start.16 = (f32[12,3,16,2]{3,0,2,1:T(8,128)S(1)}, f32[12,3,16,2]{3,0,2,1:T(8,128)S(1)}, u32[]{:S(2)}, u32[]{:S(2)}) collective-permute-start(f32[12,3,16,2]{3,0,2,1:T(8,128)S(1)} %get-tuple-element.54), channel_id=1, source_target_pairs={{0,16},{16,32},{32,48},{48,64},{64,80},{80,96},{96,112},{112,128},... | collective-permute-start | bytes 13832 | tf_op jit(solution)/shard_map/ppermute | solution.py:21
  79.2 8.6 %collective-permute-start.17 = (f32[12,3,16,2]{3,0,2,1:T(8,128)S(1)}, f32[12,3,16,2]{3,0,2,1:T(8,128)S(1)}, u32[]{:S(2)}, u32[]{:S(2)}) collective-permute-start(f32[12,3,16,2]{3,0,2,1:T(8,128)S(1)} %get-tuple-element.55), channel_id=1, source_target_pairs={{16,0},{32,16},{48,32},{64,48},{80,64},{96,80},{112,96},{128,112},... | collective-permute-start | bytes 13832 | tf_op jit(solution)/shard_map/ppermute | solution.py:24
  87.9 5.4 %collective-permute-start.18 = (f32[12,3,2,132]{3,0,2,1:T(8,128)S(1)}, f32[12,3,2,132]{3,0,2,1:T(8,128)S(1)}, u32[]{:S(2)}, u32[]{:S(2)}) collective-permute-start(f32[12,3,2,132]{3,0,2,1:T(8,128)S(1)} %get-tuple-element.6), channel_id=1, source_target_pairs={{0,1},{1,2},{2,3},{3,4},{4,5},{5,6},{6,7},{7,8},{8,9},{9,10},{10,1... | collective-permute-start | bytes 114056 | tf_op jit(solution)/shard_map/ppermute | solution.py:21
  91.7 5.6 %collective-permute-start.19 = (f32[12,3,2,132]{3,0,2,1:T(8,128)S(1)}, f32[12,3,2,132]{3,0,2,1:T(8,128)S(1)}, u32[]{:S(2)}, u32[]{:S(2)}) collective-permute-start(f32[12,3,2,132]{3,0,2,1:T(8,128)S(1)} %get-tuple-element.7), channel_id=1, source_target_pairs={{1,0},{2,1},{3,2},{4,3},{5,4},{6,5},{7,6},{8,7},{9,8},{10,9},{11,1... | collective-permute-start | bytes 114056 | tf_op jit(solution)/shard_map/ppermute | solution.py:24
